TPU v7x, 128 devices: a whole 4x4x4 slice. The times are simulated.
128 devices in a mesh: chan: 8 (over x, z_hi), row: 4 (over y), col: 4 (over z_lo, core).
Axes of the slice: x: 4, y: 4, z: 4 (z_hi: 2, z_lo: 2; z = z_hi * 2 + z_lo), core: 2. Of those that a mesh axis runs over, the one named last changes fastest.
Arguments:
- voltages: bfloat16 [2, 4, 512, 64, 1031], P(None, None, ('chan', 'row', 'col')), may hold values from -6 to 6
- window: float32 [8, 64], replicated, may hold values from 0.1 to 0.6
- kept_channels: int32 [48], replicated, may hold values from 0 to 63, as said below
Outputs:
- covariance: float32 [48, 2, 2048, 2048], P('chan', None, 'row', 'col')
Inputs may be any that keep to these rules, and one draw needn't show every extreme that they name: `kept_channels`: 48 distinct channel numbers of the 64-point transform, in any order.
All inputs are finite; a program needn't handle non-finite values.
Results may differ from a plain program's by a relative error of at most 0.0019.
Values may be sent and summed in bfloat16 or wider, within the bound.
No kernel may reach another device: no remote copies, remote signals or barrier semaphores. Data moves between devices by JAX's collectives and lax.ppermute only.
A program may use at most 128 MiB of HBM per device.

v0:
```python
import math
import jax
import jax.numpy as jnp
from jax import lax
from jax.sharding import Mesh
from jax.sharding import PartitionSpec as P

COL = ("col_0", "col_1")
CHAN_ROW_COL = ("chan", "row", "col_0", "col_1")
ROW_COL = ("row", "col_0", "col_1")


def in_order(tiles, dim):
    shape = list(tiles.shape[1:])
    shape[dim] *= tiles.shape[0]
    return jnp.moveaxis(tiles, 0, dim).reshape(shape)


def gather_in_order(shard, axes, turns):
    tiles = shard[None]
    for k in turns:
        tiles = lax.all_gather(tiles, axes[k], axis=0, tiled=True)
    current = [lax.axis_size(axes[k]) for k in reversed(turns)]
    tiles = tiles.reshape(*current, *shard.shape)
    turned = sorted(range(len(turns)), key=lambda place: turns[len(turns) - 1 - place])
    return tiles.transpose(*turned, *range(len(turns), tiles.ndim)).reshape(-1, *shard.shape)


def whole_of(shard, axes, turns, dim):
    return in_order(gather_in_order(shard, axes, turns), dim)


def cut_along(shard, dim, peers):
    shape = shard.shape
    tiles = shard.reshape(*shape[:dim], peers, shape[dim] // peers, *shape[dim + 1 :])
    return jnp.moveaxis(tiles, dim, 0)


def exchange_both(shard, axis, axes, splits, concats):
    sizes = [lax.axis_size(a) for a in axes]
    tiles = cut_along(shard, splits[0], sizes[0])
    tiles = jnp.moveaxis(cut_along(tiles, splits[1] + 1, sizes[1]), 0, 1)
    inside = tiles.shape[2:]
    tiles = tiles.reshape(-1, *inside)
    tiles = lax.all_to_all(tiles, axis, split_axis=0, concat_axis=0, tiled=True)
    tiles = in_order(tiles.reshape(*sizes, *inside), concats[0] + 1)
    return in_order(tiles, concats[1])


def phase_table(kept_channels, points):
    positions = jnp.arange(points, dtype=jnp.int32)
    phases = kept_channels[:, None] * positions[None, :] % points
    angles = phases.astype(jnp.float32) * (2.0 * math.pi / points)
    factor = 1.0 / math.sqrt(points)
    cosines = jnp.cos(angles) * factor
    sines = jnp.sin(angles) * factor
    return jnp.stack([jnp.stack([cosines, -sines]), jnp.stack([sines, cosines])])


def filter_bank(samples, window, frames):
    filtered = window[0][:, None] * samples[..., 0:frames]
    for tap_index in range(1, window.shape[0]):
        filtered = (
            filtered + window[tap_index][:, None] * samples[..., tap_index : tap_index + frames]
        )
    return filtered


def products(row_full, col_full):
    real_part = jnp.einsum(
        "bpmif,bpmjf->mij", row_full, col_full, preferred_element_type=jnp.float32
    )
    imag_part = jnp.einsum(
        "bmif,bmjf->mij", row_full[:, 1], col_full[:, 0], preferred_element_type=jnp.float32
    )
    imag_part = imag_part - jnp.einsum(
        "bmif,bmjf->mij", row_full[:, 0], col_full[:, 1], preferred_element_type=jnp.float32
    )
    inverse = 1.0 / (row_full.shape[0] * row_full.shape[4])
    return jnp.stack([real_part, imag_part], axis=1) * inverse


def correlate(pieces):
    row_part, col_part = pieces
    row_full = whole_of(row_part, COL, (0, 1), 0)
    col_full = lax.all_gather(col_part, "row", axis=0, tiled=True)
    return products(row_full, col_full)


def arrange(spectra, shape):
    return (spectra.reshape(shape), jnp.swapaxes(spectra, 1, 2).reshape(shape))


def shards(voltages, window, kept_channels):
    chan_count = lax.axis_size("chan")
    row_count = lax.axis_size("row")
    col_count = lax.axis_size(COL)
    points = window.shape[1]
    frames = voltages.shape[4] - window.shape[0] + 1
    slot_inputs = voltages.shape[2]
    per_chan = kept_channels.shape[0] // chan_count
    block_frames = frames // col_count
    samples = voltages.astype(jnp.float32)
    filtered = filter_bank(samples, window, frames)
    filtered = filtered.reshape(2, row_count, slot_inputs, points, col_count, block_frames)
    table = phase_table(kept_channels, points).reshape(2, 2, chan_count, per_chan, points)
    spectra = jnp.einsum(
        "qrsnbf,qpckn->crbpksf", filtered, table, precision=lax.Precision.HIGHEST
    ).astype(jnp.bfloat16)
    sectioned_shape = (
        chan_count,
        row_count * col_count,
        2,
        per_chan,
        1,
        1,
        slot_inputs,
        block_frames,
    )
    outgoing = arrange(spectra, sectioned_shape)
    arrived = (
        exchange_both(outgoing[0], CHAN_ROW_COL, ("chan", ROW_COL), (0, 1), (4, 5)),
        exchange_both(outgoing[1], CHAN_ROW_COL, ("chan", ROW_COL), (0, 1), (4, 5)),
    )
    arrived = jax.tree.map(lambda piece: piece.reshape(1, 2, per_chan, -1, block_frames), arrived)
    return correlate(arrived)


def solution(mesh):
    finer = Mesh(
        mesh.devices.reshape(mesh.shape["chan"], mesh.shape["row"], 2, 2),
        ("chan", "row", "col_0", "col_1"),
    )
    placed = (P(None, None, CHAN_ROW_COL, None, None), P(), P())
    return jax.shard_map(
        shards, mesh=finer, in_specs=placed, out_specs=P("chan", None, "row", COL), check_vma=False
    )
```

profile of v0, /device:TPU:1, one launch (start us, length us, event | category | flops | bytes accessed | tf_op | source)
XLA Modules:
  0.0 426.3 jit_solution(12734910430916442310)
XLA Ops:
  6.5 0.0 all-gather.4.cloned.1.call-start
  6.5 0.7 mul.173
  7.3 0.1 copy.31
  7.4 1.0 slice_bitcast_fusion.19
  8.3 0.2 fusion.31
  8.5 3.5 convert_element_type.36
  12.0 16.8 %fusion.2 = f32[2,4,4,64,1024]{4,3,2,1,0:T(8,128)} fusion(f32[2,4,4,64,1031]{4,3,2,1,0:T(8,128)S(1)} %convert_element_type.36, f32[64]{0:T(128)S(1)} %get-tuple-element.14, f32[64]{0:T(128)S(1)} %get-tuple-element.15, f32[64]{0:T(128)S(1)} %get-tuple-element.9, f32[64]{0:T(128)S(1)} %get-tuple-element.10, f32[64]{0:T(128)S(1)} %get-tuple-element.11, ...), kind=kLoop, calls=%fused_computation.4 | loop fusion | flops 31457280 | bytes 75499520 | tf_op jit(solution)/shard_map/add | solution.py:64
  28.8 10.6 %reshape.151 = f32[2,4,4,64,4,256]{5,4,3,2,1,0:T(4,128)} reshape(f32[2,4,4,64,1024]{4,3,2,1,0:T(8,128)} %fusion.2) | data formatting | bytes 16777216 | tf_op jit(solution)/shard_map/reshape | solution.py:105
  39.4 9.3 %bitcast_convert_fusion = bf16[2,8,6,4,4,4,256]{6,1,5,4,3,2,0:T(8,128)(2,1)S(1)} fusion(f32[2,4,4,64,4,256,1,1]{5,4,3,2,1,0,7,6:T(4,128)} %bitcast.102, f32[1,1,8,6,64]{4,2,0,3,1:T(8,128)S(1)} %get-tuple-element.7, f32[1,1,8,6,64]{4,2,0,3,1:T(8,128)S(1)} %get-tuple-element.6, f32[1,1,8,6,64]{4,2,0,3,1:T(8,128)S(1)} %get-tuple-element.5), kind=kOutput, calls=%fused_computation.28 | convolution fusion | flops 2417528832 | bytes 11571200 | tf_op jit(solution)/shard_map/qrsnbf,qpckn->crbpksf/dot_general | solution.py:107
  48.7 2.4 copy.33
  51.1 52.5 %all_to_all.10 = bf16[128,1,1,2,6,1,1,4,256]{8,7,4,3,6,5,2,1,0:T(4,128)(2,1)S(1)} all-to-all(bf16[128,1,1,2,6,1,1,4,256]{8,7,4,3,6,5,2,1,0:T(4,128)(2,1)S(1)} %bitcast.101), channel_id=1, replica_groups=mesh['chan'=8,'row'=4,'col_0'=2,'col_1'=2] {'chan','row','col_0','col_1'}, dimensions={0} | all-to-all | bytes 6291456 | tf_op jit(solution)/shard_map/all_to_all | solution.py:45
  103.7 3.3 copy.35
  106.9 2.2 copy.36
  109.1 0.0 all-gather.4.cloned.1.call-update
  109.1 0.0 all-gather.6.cloned.1.call-start
  109.2 79.7 %all-gather.4.cloned.1.call-done = bf16[2,1,2,6,512,256]{5,4,3,2,1,0:T(8,128)(2,1)} async-done(((bf16[1,1,2,6,512,256]{5,4,3,2,1,0:T(8,128)(2,1)}), bf16[2,1,2,6,512,256]{5,4,3,2,1,0:T(8,128)(2,1)}) %all-gather.4.cloned.1.call-update) | async-done | bytes 6291472 | tf_op jit(solution)/shard_map/all_gather | solution.py:22
  188.9 0.0 all-gather.6.cloned.1.call-update
  188.9 0.0 all-gather.8.cloned.1.call-start
  188.9 2.4 copy.38
  191.4 50.3 %all_to_all.11 = bf16[128,1,1,2,6,1,1,4,256]{8,7,4,3,6,5,2,1,0:T(4,128)(2,1)S(1)} all-to-all(bf16[128,1,1,2,6,1,1,4,256]{8,7,4,3,6,5,2,1,0:T(4,128)(2,1)S(1)} %bitcast.99), channel_id=1, replica_groups=mesh['chan'=8,'row'=4,'col_0'=2,'col_1'=2] {'chan','row','col_0','col_1'}, dimensions={0} | all-to-all | bytes 6291456 | tf_op jit(solution)/shard_map/all_to_all | solution.py:45
  241.6 1.7 copy.40
  243.4 3.0 reshape_reshape.7
  246.4 0.0 all-gather.8.cloned.1.call-update
  246.4 0.0 all-gather.6.cloned.1.call-done
  246.5 10.8 %copy.37 = bf16[2,2,1,2,6,512,256]{6,5,3,4,1,0,2:T(8,128)(2,1)} copy(bf16[2,2,1,2,6,512,256]{6,5,4,3,0,1,2:T(8,128)(2,1)} %bitcast.91) | data formatting | bytes 25165824 | tf_op jit(solution)/shard_map/transpose | solution.py:26
  257.3 104.5 %all-gather.8.cloned.1.call-done = bf16[4,2,6,512,256]{4,3,2,1,0:T(8,128)(2,1)} async-done(((bf16[1,2,6,512,256]{4,3,2,1,0:T(8,128)(2,1)}), bf16[4,2,6,512,256]{4,3,2,1,0:T(8,128)(2,1)}) %all-gather.8.cloned.1.call-update) | async-done | bytes 12582928 | tf_op jit(solution)/shard_map/all_gather | solution.py:86
  361.8 10.6 %fusion.11 = f32[6,512,512,1]{2,1,0,3:T(8,128)} fusion(bf16[4,2,6,512,256]{4,3,2,1,0:T(8,128)(2,1)} %all-gather.8.cloned.1.call-done, bf16[4,2,6,512,256]{4,3,1,2,0:T(8,128)(2,1)} %bitcast.92), kind=kOutput, calls=%fused_computation.21 | convolution fusion | flops 3221225472 | bytes 18874368 | tf_op jit(solution)/shard_map/bmif,bmjf->mij/dot_general | solution.py:76
  372.4 15.0 %fusion.16 = f32[6,1,512,512]{3,2,0,1:T(8,128)} fusion(bf16[4,2,6,512,256]{4,3,1,2,0:T(8,128)(2,1)} %bitcast.93, bf16[4,2,6,512,256]{4,3,2,1,0:T(8,128)(2,1)} %all-gather.8.cloned.1.call-done), kind=kOutput, calls=%fused_computation.29 | convolution fusion | flops 6442450944 | bytes 31457280 | tf_op jit(solution)/shard_map/bpmif,bpmjf->mij/dot_general | solution.py:70
  387.4 12.6 %fusion.13 = f32[6,1,512,512]{3,2,0,1:T(8,128)} fusion(f32[6,512,512,1]{2,1,0,3:T(8,128)} %fusion.11, bf16[4,2,6,512,256]{4,3,2,1,0:T(8,128)(2,1)} %all-gather.8.cloned.1.call-done, bf16[4,2,6,512,256]{4,3,1,2,0:T(8,128)(2,1)} %bitcast.94), kind=kOutput, calls=%fused_computation.27 | convolution fusion | flops 3222798336 | bytes 25165824 | tf_op jit(solution)/shard_map/bmif,bmjf->mij/dot_general | solution.py:73
  400.0 0.0 copy-done
  400.0 8.9 %maximum_multiply_fusion = f32[6,2,512,512]{3,2,0,1:T(8,128)} fusion(f32[6,1,512,512]{3,2,0,1:T(8,128)} %fusion.13, f32[6,1,512,512]{3,2,0,1:T(8,128)S(1)} %copy-done), kind=kLoop, calls=%fused_computation | loop fusion | flops 6291456 | bytes 25165824 | tf_op jit(solution)/shard_map/mul | solution.py:80
  408.9 10.9 %copy.44 = f32[6,2,512,512]{3,2,1,0:T(8,128)} copy(f32[6,2,512,512]{3,2,0,1:T(8,128)} %maximum_multiply_fusion) | data formatting | bytes 25165824 | tf_op jit(solution)/shard_map/mul | solution.py:80
  (1 shorter events, 0.0 us)
Async XLA Ops:
  6.5 182.3 %all-gather.4.cloned.1.call-start = ((), (), s32[]{:S(2)}) async-start(), calls=%async_computation.2 | async-start | bytes 9437184 | tf_op jit(solution)/shard_map/all_gather | solution.py:22
  109.1 137.3 %all-gather.6.cloned.1.call-start = ((), (), s32[]{:S(2)}) async-start(), calls=%async_computation.3 | async-start | bytes 18874368 | tf_op jit(solution)/shard_map/all_gather | solution.py:22
  188.9 172.9 %all-gather.8.cloned.1.call-start = ((), (), s32[]{:S(2)}) async-start(), calls=%async_computation.4 | async-start | bytes 15728640 | tf_op jit(solution)/shard_map/all_gather | solution.py:86
  387.4 12.6 %copy-start = (f32[6,1,512,512]{3,2,0,1:T(8,128)S(1)}, f32[6,1,512,512]{3,2,0,1:T(8,128)}, u32[]{:S(2)}) copy-start(f32[6,1,512,512]{3,2,0,1:T(8,128)} %fusion.16) | copy-start | bytes 18874372
Sparse Core Ops, SparseCore 0:
  109.2 79.5 all-gather.3
  190.5 28.9 all-gather.5
  246.6 115.1 all-gather.7
where the time goes:
time: 427 us; the launch traced here: 426 us
  waiting for transfers between devices  184 us (43%)
  blocking collectives  103 us (24%)
  local copies, waits for them, and re-layouts  49.1 us (11%)
  matrix products  47.5 us (11%)
  other arithmetic  29.4 us (7%)
  between operations  13.2 us (3%)
    all_gather x1, waiting for transfers between devices, correlate(): col_full = lax.all_gather(col_part, 'row', axis=0, tiled=True)  105 us
    all_to_all x2, blocking collectives, exchange_both(): tiles = lax.all_to_all(tiles, axis, split_axis=0, concat_axis=0, tiled=True)  103 us
    all_gather x2, waiting for transfers between devices, gather_in_order(): tiles = lax.all_gather(tiles, axes[k], axis=0, tiled=True)  79.7 us
    add x1, other arithmetic, filter_bank(): filtered + window[tap_index][:, None] * samples[..., tap_index:tap_index...  16.8 us
    dot_general x1, matrix products, products(): jnp.einsum('bpmif,bpmjf->mij', row_full, col_full, preferred_element_type...  15 us
    dot_general x1, matrix products, products(): jnp.einsum('bmif,bmjf->mij', row_full[:, 1], col_full[:, 0], preferred_el...  12.6 us
    mul x1, local copies, waits for them, and re-layouts, products(): return jnp.stack([real_part, imag_part], axis=1) * inverse  10.9 us
    transpose x1, local copies, waits for them, and re-layouts, gather_in_order(): tiles.transpose(*turned, *range(len(turns), tiles.ndim))  10.8 us
  transfers between devices with their start and end apart: 3, of which 2 were waited for; matrix products, arithmetic and copies ran while one was open for 4% of the time, Pallas kernels for 0%

commit v1 on v0

--- a/solution.py
+++ b/solution.py
@@ -83,7 +83,9 @@
 def correlate(pieces):
     row_part, col_part = pieces
     row_full = whole_of(row_part, COL, (0, 1), 0)
-    col_full = lax.all_gather(col_part, "row", axis=0, tiled=True)
+    col_full = jnp.concatenate(
+        lax.all_to_all(jnp.stack([col_part] * lax.axis_size("row")), "row", 0, 0), axis=0
+    )
     return products(row_full, col_full)
 
 

time: 427 us -> 458 us (1.073)
  waiting for transfers between devices: 184 us -> 207 us
  starting transfers between devices: 0.08 us -> 6.56 us
  matrix products: 47.5 us -> 42.6 us
    all_to_all x0 -> x1, waiting for transfers between devices: none -> 127 us  [correlate(): lax.all_to_all(jnp.stack([col_part] * lax.axis_size('row')), 'row', 0, 0)]
    all_gather x1 -> x0, waiting for transfers between devices: 105 us -> none  [correlate(): col_full = lax.all_gather(col_part, 'row', axis=0, tiled=True)]
    all_to_all x0 -> x1, starting transfers between devices: none -> 6.52 us  [correlate(): lax.all_to_all(jnp.stack([col_part] * lax.axis_size('row')), 'row', 0, 0)]
  transfers between devices with their start and end apart: 3 -> 3, of which waited for: 2 -> 2; matrix products, arithmetic and copies ran while one was open for 4% -> 5% of each run, Pallas kernels for 0% -> 0%
where the time goes in v1:
time: 458 us; the launch traced here: 457 us
  waiting for transfers between devices  207 us (45%)
  blocking collectives  103 us (22%)
  local copies, waits for them, and re-layouts  53.4 us (12%)
  matrix products  42.6 us (9%)
  other arithmetic  31.3 us (7%)
  between operations  13.5 us (3%)
  starting transfers between devices  6.56 us (1%)
    all_to_all x1, waiting for transfers between devices, correlate(): lax.all_to_all(jnp.stack([col_part] * lax.axis_size('row')), 'row', 0, 0)  127 us
    all_to_all x2, blocking collectives, exchange_both(): tiles = lax.all_to_all(tiles, axis, split_axis=0, concat_axis=0, tiled=True)  103 us
    all_gather x2, waiting for transfers between devices, gather_in_order(): tiles = lax.all_gather(tiles, axes[k], axis=0, tiled=True)  79.7 us
    add x1, other arithmetic, filter_bank(): filtered + window[tap_index][:, None] * samples[..., tap_index:tap_index...  16.8 us
    dot_general x1, matrix products, products(): jnp.einsum('bpmif,bpmjf->mij', row_full, col_full, preferred_element_type...  14.9 us
    dot_general x1, matrix products, products(): jnp.einsum('bmif,bmjf->mij', row_full[:, 1], col_full[:, 0], preferred_el...  10.9 us
    mul x1, local copies, waits for them, and re-layouts, products(): return jnp.stack([real_part, imag_part], axis=1) * inverse  10.9 us
    mul x1, other arithmetic, products(): return jnp.stack([real_part, imag_part], axis=1) * inverse  10.8 us
  transfers between devices with their start and end apart: 3, of which 2 were waited for; matrix products, arithmetic and copies ran while one was open for 5% of the time, Pallas kernels for 0%

profile of v1, /device:TPU:1, one launch (start us, length us, event | category | flops | bytes accessed | tf_op | source)
XLA Modules:
  0.0 457.1 jit_solution(256704139636883759)
XLA Ops:
  6.5 0.0 all-gather.3.cloned.1.call-start
  6.5 1.0 slice_bitcast_fusion.19
  7.5 3.5 convert_element_type.36
  11.0 16.8 %fusion = f32[2,4,4,64,1024]{4,3,2,1,0:T(8,128)} fusion(f32[2,4,4,64,1031]{4,3,2,1,0:T(8,128)S(1)} %convert_element_type.36, f32[64]{0:T(128)S(1)} %get-tuple-element.14, f32[64]{0:T(128)S(1)} %get-tuple-element.15, f32[64]{0:T(128)S(1)} %get-tuple-element.9, f32[64]{0:T(128)S(1)} %get-tuple-element.10, f32[64]{0:T(128)S(1)} %get-tuple-element.11, ...), kind=kLoop, calls=%fused_computation.2 | loop fusion | flops 31457280 | bytes 75499520 | tf_op jit(solution)/shard_map/add | solution.py:64
  27.8 10.6 %reshape.158 = f32[2,4,4,64,4,256]{5,4,3,2,1,0:T(4,128)} reshape(f32[2,4,4,64,1024]{4,3,2,1,0:T(8,128)} %fusion) | data formatting | bytes 16777216 | tf_op jit(solution)/shard_map/reshape | solution.py:107
  38.4 0.0 copy-done
  38.4 0.1 mul.173
  38.5 0.1 copy.30
  38.6 0.2 fusion.26
  38.8 9.3 %bitcast_convert_fusion = bf16[2,8,6,4,4,4,256]{6,1,5,4,3,2,0:T(8,128)(2,1)S(1)} fusion(f32[2,4,4,64,4,256,1,1]{5,4,3,2,1,0,7,6:T(4,128)} %bitcast.101, f32[1,1,8,6,64]{4,2,0,3,1:T(8,128)S(1)} %get-tuple-element.7, f32[1,1,8,6,64]{4,2,0,3,1:T(8,128)S(1)} %get-tuple-element.6, f32[1,1,8,6,64]{4,2,0,3,1:T(8,128)S(1)} %get-tuple-element.5), kind=kOutput, calls=%fused_computation.26 | convolution fusion | flops 2417528832 | bytes 11571200 | tf_op jit(solution)/shard_map/qrsnbf,qpckn->crbpksf/dot_general | solution.py:109
  48.1 2.4 copy.32
  50.5 52.5 %all_to_all.15 = bf16[128,1,1,2,6,1,1,4,256]{8,7,4,3,6,5,2,1,0:T(4,128)(2,1)S(1)} all-to-all(bf16[128,1,1,2,6,1,1,4,256]{8,7,4,3,6,5,2,1,0:T(4,128)(2,1)S(1)} %bitcast.100), channel_id=1, replica_groups=mesh['chan'=8,'row'=4,'col_0'=2,'col_1'=2] {'chan','row','col_0','col_1'}, dimensions={0} | all-to-all | bytes 6291456 | tf_op jit(solution)/shard_map/all_to_all | solution.py:45
  103.0 3.3 copy.34
  106.3 2.2 copy.35
  108.5 0.0 all-gather.3.cloned.1.call-update
  108.5 0.0 all-gather.5.cloned.1.call-start
  108.5 79.7 %all-gather.3.cloned.1.call-done = bf16[2,1,2,6,512,256]{5,4,3,2,1,0:T(8,128)(2,1)} async-done(((bf16[1,1,2,6,512,256]{5,4,3,2,1,0:T(8,128)(2,1)}), bf16[2,1,2,6,512,256]{5,4,3,2,1,0:T(8,128)(2,1)}) %all-gather.3.cloned.1.call-update) | async-done | bytes 6291472 | tf_op jit(solution)/shard_map/all_gather | solution.py:22
  188.2 0.0 all-gather.5.cloned.1.call-update
  188.3 2.4 copy.37
  190.7 50.3 %all_to_all.16 = bf16[128,1,1,2,6,1,1,4,256]{8,7,4,3,6,5,2,1,0:T(4,128)(2,1)S(1)} all-to-all(bf16[128,1,1,2,6,1,1,4,256]{8,7,4,3,6,5,2,1,0:T(4,128)(2,1)S(1)} %bitcast.97), channel_id=1, replica_groups=mesh['chan'=8,'row'=4,'col_0'=2,'col_1'=2] {'chan','row','col_0','col_1'}, dimensions={0} | all-to-all | bytes 6291456 | tf_op jit(solution)/shard_map/all_to_all | solution.py:45
  241.0 3.3 copy.39
  244.2 0.5 copy.40
  244.8 6.3 %stack.30 = bf16[4,1,2,6,512,256]{5,4,2,3,1,0:T(8,128)(2,1)} broadcast(bf16[2,6,512,256]{3,2,0,1:T(8,128)(2,1)S(1)} %copy.40), dimensions={2,3,4,5} | broadcast | bytes 15728640 | tf_op jit(solution)/shard_map/stack | solution.py:87
  251.0 6.5 %all-to-all-start.2 = ((bf16[4,1,2,6,512,256]{5,4,2,3,1,0:T(8,128)(2,1)}), bf16[4,1,2,6,512,256]{5,4,2,3,1,0:T(8,128)(2,1)}, u32[]{:S(2)}, u32[]{:S(2)}) async-start(bf16[4,1,2,6,512,256]{5,4,2,3,1,0:T(8,128)(2,1)} %stack.30), calls=%async_computation.2 | async-start | bytes 25165824 | tf_op jit(solution)/shard_map/all_to_all | solution.py:87
  257.6 0.0 all-gather.5.cloned.1.call-done
  257.6 10.5 %copy.36 = bf16[2,2,1,2,6,512,256]{6,5,3,4,1,0,2:T(8,128)(2,1)} copy(bf16[2,2,1,2,6,512,256]{6,5,4,3,0,1,2:T(8,128)(2,1)} %bitcast.89) | data formatting | bytes 25165824 | tf_op jit(solution)/shard_map/transpose | solution.py:26
  268.1 127.2 %all-to-all-done.2 = bf16[4,1,2,6,512,256]{5,4,2,3,1,0:T(8,128)(2,1)} async-done(((bf16[4,1,2,6,512,256]{5,4,2,3,1,0:T(8,128)(2,1)}), bf16[4,1,2,6,512,256]{5,4,2,3,1,0:T(8,128)(2,1)}, u32[]{:S(2)}, u32[]{:S(2)}) %all-to-all-start.2) | async-done | bytes 12582944 | tf_op jit(solution)/shard_map/all_to_all | solution.py:87
  395.2 7.5 %fusion.9 = f32[6,512,512,1]{2,1,0,3:T(8,128)S(1)} fusion(bf16[4,2,6,512,256]{4,3,1,2,0:T(8,128)(2,1)} %bitcast.32, bf16[4,2,6,512,256]{4,3,1,2,0:T(8,128)(2,1)} %bitcast.90), kind=kOutput, calls=%fused_computation.19 | convolution fusion | flops 3221225472 | bytes 18874368 | tf_op jit(solution)/shard_map/bmif,bmjf->mij/dot_general | solution.py:76
  402.7 10.9 %fusion.11 = f32[6,1,512,512]{3,2,0,1:T(8,128)} fusion(f32[6,512,512,1]{2,1,0,3:T(8,128)S(1)} %fusion.9, bf16[4,2,6,512,256]{4,3,1,2,0:T(8,128)(2,1)} %bitcast.32, bf16[4,2,6,512,256]{4,3,1,2,0:T(8,128)(2,1)} %bitcast.91), kind=kOutput, calls=%fused_computation.25 | convolution fusion | flops 3222798336 | bytes 25165824 | tf_op jit(solution)/shard_map/bmif,bmjf->mij/dot_general | solution.py:73
  413.6 14.9 %convolution_bitcast_fusion = f32[6,1,512,512]{3,2,0,1:T(8,128)} fusion(bf16[4,2,6,512,256]{4,3,1,2,0:T(8,128)(2,1)} %bitcast.92, bf16[4,1,2,6,512,256]{5,4,2,3,1,0:T(8,128)(2,1)} %all-to-all-done.2), kind=kOutput, calls=%fused_computation.27 | convolution fusion | flops 6442450944 | bytes 31457280 | tf_op jit(solution)/shard_map/bpmif,bpmjf->mij/dot_general | solution.py:70
  428.5 10.8 %maximum_multiply_fusion = f32[6,2,512,512]{3,2,0,1:T(8,128)} fusion(f32[6,1,512,512]{3,2,0,1:T(8,128)} %fusion.11, f32[6,1,512,512]{3,2,0,1:T(8,128)} %convolution_bitcast_fusion), kind=kLoop, calls=%fused_computation | loop fusion | flops 6291456 | bytes 25165824 | tf_op jit(solution)/shard_map/mul | solution.py:80
  439.4 10.9 %copy.41 = f32[6,2,512,512]{3,2,1,0:T(8,128)} copy(f32[6,2,512,512]{3,2,0,1:T(8,128)} %maximum_multiply_fusion) | data formatting | bytes 25165824 | tf_op jit(solution)/shard_map/mul | solution.py:80
  (1 shorter events, 0.0 us)
Async XLA Ops:
  6.5 181.7 %all-gather.3.cloned.1.call-start = ((), (), s32[]{:S(2)}) async-start(), calls=%async_computation.3 | async-start | bytes 9437184 | tf_op jit(solution)/shard_map/all_gather | solution.py:22
  27.8 10.6 %copy-start = (s32[48]{0:T(128)S(1)}, s32[48]{0:T(128)}, u32[]{:S(2)}) copy-start(s32[48]{0:T(128)} %param.5) | copy-start | bytes 580
  108.5 149.1 %all-gather.5.cloned.1.call-start = ((), (), s32[]{:S(2)}) async-start(), calls=%async_computation.4 | async-start | bytes 18874368 | tf_op jit(solution)/shard_map/all_gather | solution.py:22
  251.0 144.2 %all-to-all-start.2 = ((bf16[4,1,2,6,512,256]{5,4,2,3,1,0:T(8,128)(2,1)}), bf16[4,1,2,6,512,256]{5,4,2,3,1,0:T(8,128)(2,1)}, u32[]{:S(2)}, u32[]{:S(2)}) async-start(bf16[4,1,2,6,512,256]{5,4,2,3,1,0:T(8,128)(2,1)} %stack.30), calls=%async_computation.2 | async-start | bytes 25165824 | tf_op jit(solution)/shard_map/all_to_all | solution.py:87
Sparse Core Ops, SparseCore 0:
  108.6 79.5 all-gather.2
  189.9 28.9 all-gather.4
